TPU v7x, 512 devices: a whole 4x8x8 slice. The times are simulated.
512 devices in a mesh: enc: 8 (over x, core), row: 4 (over y_lo), col: 16 (over z, y_hi).
Axes of the slice: x: 4, y: 8 (y_hi: 2, y_lo: 4; y = y_hi * 4 + y_lo), z: 8, core: 2. Of those that a mesh axis runs over, the one named last changes fastest.
Arguments:
- queries: bfloat16 [10240, 3072], P(('row', 'col'), 'enc'), may hold values from -150 to 150
- self_keys: bfloat16 [10240, 3072], P(('row', 'col'), 'enc'), may hold values from -150 to 150
- self_values: bfloat16 [10240, 3072], P(('row', 'col'), 'enc'), may hold values from -6 to 6
- positions: int32 [10240, 3], P(('row', 'col')), may hold values from 0 to 63, as said below
- query_gain: float32 [3072], P('enc'), may hold values from 1.3 to 2
- key_gain: float32 [3072], P('enc'), may hold values from 1.3 to 2
- context_keys: bfloat16 [128, 3072], P(('enc', 'row')), may hold values from -150 to 150
- context_values: bfloat16 [128, 3072], P(('enc', 'row')), may hold values from -6 to 6
- context_gain: float32 [3072], replicated, may hold values from 0.1 to 1.9
- image_cotangent: bfloat16 [10240, 3072], P(('row', 'col'), 'enc'), may hold values from -6 to 6
Outputs:
- self_mixed: bfloat16 [10240, 3072], P(('row', 'col'), 'enc')
- image_mixed: bfloat16 [10240, 3072], P(('row', 'col'), 'enc')
- grad_context_keys: float32 [128, 3072], P(('enc', 'row'))
- grad_context_values: float32 [128, 3072], P(('enc', 'row'))
Inputs may be any that keep to these rules, and one draw needn't show every extreme that they name: `positions`: each (frame, patch row, patch column) of the 5 x 32 x 64 grid appears once; the tokens of one device form one tile of 8 x 4 patches in every frame, in order of frame, row, column; which tile lies on which device is drawn.
All inputs are finite; a program needn't handle non-finite values.
Results may differ from a plain program's by a relative error of at most 0.002.
The roundings to bfloat16 on the way count: a program that leaves them out, or rounds other values in their place, can miss the bound.
Values may be sent and summed in bfloat16 or wider, within the bound.
A program may use at most 128 MiB of HBM per device.

v0:
```python
import jax
import jax.numpy as jnp
from jax import lax
from jax.sharding import PartitionSpec as P

HEAD_DIM = 128


eps = 1e-06


def rope_angles(positions):
    half = HEAD_DIM // 2
    part_side = HEAD_DIM // 6
    part_time = half - 2 * part_side
    freq_time = 1.0 / 10000.0 ** (jnp.arange(part_time, dtype=jnp.float32) * 2.0 / (2 * part_time))
    freq_side = 1.0 / 10000.0 ** (jnp.arange(part_side, dtype=jnp.float32) * 2.0 / (2 * part_side))
    zeros_side = jnp.zeros((part_side,), jnp.float32)
    zeros_time = jnp.zeros((part_time,), jnp.float32)
    time_row = jnp.concatenate([freq_time, zeros_side, zeros_side])
    height_row = jnp.concatenate([zeros_time, freq_side, zeros_side])
    width_row = jnp.concatenate([zeros_time, zeros_side, freq_side])
    coords = positions.astype(jnp.float32)
    return coords[:, 0:1] * time_row + coords[:, 1:2] * height_row + coords[:, 2:3] * width_row


def pair_turn():
    indices = jnp.arange(HEAD_DIM)
    rows_index = indices[:, None]
    cols_index = indices[None, :]
    plus_entry = (cols_index == rows_index + 1) & (rows_index % 2 == 0)
    minus_entry = (rows_index == cols_index + 1) & (cols_index % 2 == 0)
    return jnp.where(plus_entry, 1.0, jnp.where(minus_entry, -1.0, 0.0)).astype(jnp.float32)


def rotate(normed, angles):
    row_count = normed.shape[0]
    heads_here = normed.shape[1] // HEAD_DIM
    turned = jnp.dot(
        normed.reshape(row_count * heads_here, HEAD_DIM),
        pair_turn(),
        precision=lax.Precision.HIGHEST,
    )
    turned = turned.reshape(row_count, heads_here, HEAD_DIM)
    cosine = jnp.repeat(jnp.cos(angles), 2, axis=1)[:, None, :]
    sine = jnp.repeat(jnp.sin(angles), 2, axis=1)[:, None, :]
    return normed.reshape(row_count, heads_here, HEAD_DIM) * cosine + turned * sine


def per_device(
    queries,
    self_keys,
    self_values,
    positions,
    query_gain,
    key_gain,
    context_keys,
    context_values,
    context_gain,
    image_cotangent,
):
    rows_here = queries.shape[0]
    local_width = queries.shape[1]
    heads_here = local_width // HEAD_DIM
    score_scale = HEAD_DIM ** (-0.5)
    query_wide = queries.astype(jnp.float32)
    key_wide = self_keys.astype(jnp.float32)
    query_total, key_total = lax.psum(
        (jnp.sum(query_wide * query_wide, axis=1), jnp.sum(key_wide * key_wide, axis=1)), "enc"
    )
    full_width = local_width * lax.axis_size("enc")
    query_normed = query_wide * lax.rsqrt(query_total[:, None] / full_width + eps) * query_gain
    key_normed = key_wide * lax.rsqrt(key_total[:, None] / full_width + eps) * key_gain
    angles = rope_angles(positions)
    query_turned = rotate(query_normed, angles).astype(jnp.bfloat16)
    key_turned = rotate(key_normed, angles).astype(jnp.bfloat16).reshape(rows_here, local_width)
    peak_now = jnp.full((heads_here, rows_here), -1e30, jnp.float32)
    accumulated = jnp.zeros((rows_here, heads_here, HEAD_DIM), jnp.float32)
    key_piece = lax.all_gather(key_turned, ("row", "col"), axis=0, tiled=True)
    value_piece = lax.all_gather(self_values, ("row", "col"), axis=0, tiled=True)
    key_count = key_piece.shape[0]
    key_heads = key_piece.reshape(key_count, heads_here, HEAD_DIM)
    value_heads = value_piece.reshape(key_count, heads_here, HEAD_DIM)
    scores = (
        jnp.einsum("qhd,khd->hqk", query_turned, key_heads, preferred_element_type=jnp.float32)
        * score_scale
    )
    newest = jnp.maximum(peak_now, jnp.max(scores, axis=2))
    shrink = jnp.exp(peak_now - newest)
    weights = jnp.exp(scores - newest[:, :, None])
    weight_sum = jnp.sum(weights, axis=2)
    update = jnp.einsum(
        "hqk,khd->qhd",
        weights.astype(jnp.bfloat16),
        value_heads,
        preferred_element_type=jnp.float32,
    )
    accumulated = accumulated * shrink.T[:, :, None] + update
    peak_now, weight_sum, accumulated = (newest, weight_sum, accumulated)
    self_out = (
        (accumulated / weight_sum.T[:, :, None])
        .astype(jnp.bfloat16)
        .reshape(rows_here, local_width)
    )
    query_plain = query_normed.astype(jnp.bfloat16).reshape(rows_here, heads_here, HEAD_DIM)
    context_wide = context_keys.astype(jnp.float32)
    context_recip = lax.rsqrt(jnp.mean(context_wide * context_wide, axis=1, keepdims=True) + eps)
    context_normed = (context_wide * context_recip * context_gain).astype(jnp.bfloat16)
    relayed_keys, relayed_values = (
        lax.all_to_all(context_normed, "enc", split_axis=1, concat_axis=0, tiled=True),
        lax.all_to_all(context_values, "enc", split_axis=1, concat_axis=0, tiled=True),
    )
    cross_keys, cross_values = (
        lax.all_gather(relayed_keys, "row", axis=0, tiled=True),
        lax.all_gather(relayed_values, "row", axis=0, tiled=True),
    )
    context_count = cross_keys.shape[0]
    cross_key_heads = cross_keys.reshape(context_count, heads_here, HEAD_DIM)
    cross_value_heads = cross_values.reshape(context_count, heads_here, HEAD_DIM)
    image_scores = (
        jnp.einsum("qhd,chd->hqc", query_plain, cross_key_heads, preferred_element_type=jnp.float32)
        * score_scale
    )
    image_peak = jnp.max(image_scores, axis=2, keepdims=True)
    image_weights = jnp.exp(image_scores - image_peak)
    probs = image_weights / jnp.sum(image_weights, axis=2, keepdims=True)
    probs_low = probs.astype(jnp.bfloat16)
    image_out = jnp.einsum(
        "hqc,chd->qhd", probs_low, cross_value_heads, preferred_element_type=jnp.float32
    )
    image_out = image_out.astype(jnp.bfloat16).reshape(rows_here, local_width)
    cotangent = image_cotangent.reshape(rows_here, heads_here, HEAD_DIM)
    grad_values = jnp.einsum(
        "hqc,qhd->chd", probs_low, cotangent, preferred_element_type=jnp.float32
    ).reshape(context_count, local_width)
    grad_probs = jnp.einsum(
        "qhd,chd->hqc", cotangent, cross_value_heads, preferred_element_type=jnp.float32
    )
    inner = jnp.sum(probs * grad_probs, axis=2, keepdims=True)
    grad_scores = (probs * (grad_probs - inner)).astype(jnp.bfloat16)
    grad_keys = (
        jnp.einsum("hqc,qhd->chd", grad_scores, query_plain, preferred_element_type=jnp.float32)
        * score_scale
    )
    grad_keys = grad_keys.reshape(context_count, local_width)
    whole_keys, whole_values = lax.psum((grad_keys, grad_values), ("row", "col"))
    row_block = context_count // lax.axis_size("row")
    first_row = lax.axis_index("row") * row_block
    summed_keys = lax.dynamic_slice_in_dim(whole_keys, first_row, row_block, 0)
    summed_values = lax.dynamic_slice_in_dim(whole_values, first_row, row_block, 0)
    back_keys, back_values = (
        lax.all_to_all(summed_keys, "enc", split_axis=0, concat_axis=1, tiled=True),
        lax.all_to_all(summed_values, "enc", split_axis=0, concat_axis=1, tiled=True),
    )
    scaled_grad = context_gain * back_keys
    grad_keys_in = context_recip * scaled_grad - context_wide * context_recip**3 * jnp.mean(
        context_wide * scaled_grad, axis=1, keepdims=True
    )
    return (self_out, image_out, grad_keys_in, back_values)


def solution(mesh):
    return jax.shard_map(
        per_device,
        mesh=mesh,
        in_specs=(
            P(("row", "col"), "enc"),
            P(("row", "col"), "enc"),
            P(("row", "col"), "enc"),
            P(("row", "col"), None),
            P("enc"),
            P("enc"),
            P(("enc", "row"), None),
            P(("enc", "row"), None),
            P(),
            P(("row", "col"), "enc"),
        ),
        out_specs=(
            P(("row", "col"), "enc"),
            P(("row", "col"), "enc"),
            P(("enc", "row"), None),
            P(("enc", "row"), None),
        ),
        check_vma=False,
    )
```

profile of v0, /device:TPU:6, one launch (start us, length us, event | category | flops | bytes accessed | tf_op | source)
XLA Modules:
  0.0 1205.5 jit_solution(12245201308022729796)
XLA Ops:
  7.2 0.9 fusion.65
  8.1 1.4 fusion.67
  9.5 9.1 all-to-all-start
  19.3 1.0 fusion.30
  20.4 1.0 fusion.34
  21.4 10.7 all-reduce.2
  32.1 1.0 fusion.41
  33.2 8.0 all-to-all-start.1
  41.2 13.3 %all_gather.14 = bf16[128,384]{1,0:T(8,128)(2,1)S(1)} all-gather(bf16[32,384]{1,0:T(8,128)(2,1)S(1)} %all_to_all.59), channel_id=1, replica_groups=mesh['enc'=8,'row'=4,'col'=16] {'row'}, dimensions={0}, use_global_device_ids=true | all-gather | bytes 122880 | tf_op jit(solution)/shard_map/all_gather | solution.py:114
  54.7 13.3 %all_gather.15 = bf16[128,384]{1,0:T(8,128)(2,1)S(1)} all-gather(bf16[32,384]{1,0:T(8,128)(2,1)S(1)} %all_to_all.63), channel_id=1, replica_groups=mesh['enc'=8,'row'=4,'col'=16] {'row'}, dimensions={0}, use_global_device_ids=true | all-gather | bytes 122880 | tf_op jit(solution)/shard_map/all_gather | solution.py:115
  68.5 1.0 fusion.42
  69.9 1.2 convolution_multiply_fusion.3
  71.1 0.9 copy.66
  72.0 0.8 copy.68
  73.7 1.4 fusion.20
  77.1 152.7 %all-reduce.5.cloned.1.call-done = (f32[128,384]{1,0:T(8,128)}, f32[128,384]{1,0:T(8,128)}) async-done(((f32[128,384]{1,0:T(8,128)}, f32[128,384]{1,0:T(8,128)}), (f32[128,384]{1,0:T(8,128)}, f32[128,384]{1,0:T(8,128)})) %all-reduce.5.cloned.1.call-update) | async-done | bytes 393232 | tf_op jit(solution)/shard_map/psum | solution.py:146
  229.8 0.8 constant_dynamic-slice_fusion
  231.2 4.8 all-to-all-start.3
  236.0 0.8 constant_dynamic-slice_fusion.1
  237.5 2.0 all-to-all-done.3
  239.5 5.4 all-to-all-start.2
  244.8 0.9 fusion.19
  246.4 1.9 all-to-all-done.2
  248.3 0.9 fusion.70
  249.2 1.4 fusion.69
  250.6 437.8 %all-gather.3.cloned.1.call-done = bf16[10240,384]{1,0:T(8,128)(2,1)} async-done(((bf16[160,384]{1,0:T(8,128)(2,1)}), bf16[10240,384]{1,0:T(8,128)(2,1)}) %all-gather.3.cloned.1.call-update) | async-done | bytes 7864336 | tf_op jit(solution)/shard_map/all_gather | solution.py:79
  688.5 10.7 copy.50
  699.2 12.7 %multiply_reduce_fusion = (f32[3,160]{1,0:T(4,128)S(1)}, f32[3,160,10240]{2,1,0:T(8,128)}) fusion(bf16[160,3,128]{2,0,1:T(8,128)(2,1)S(1)} %fusion.17, bf16[10240,3,128]{0,2,1:T(8,128)(2,1)} %bitcast.128), kind=kOutput, calls=%fused_computation.2 | convolution fusion | flops 1268121088 | bytes 27649920 | tf_op jit(solution)/shard_map/qhd,khd->hqk/dot_general | solution.py:85
  711.9 10.0 fusion.1
  721.9 453.0 %all-gather.5.cloned.1.call-done = bf16[10240,384]{1,0:T(8,128)(2,1)} async-done(((bf16[160,384]{1,0:T(8,128)(2,1)}), bf16[10240,384]{1,0:T(8,128)(2,1)}) %all-gather.5.cloned.1.call-update) | async-done | bytes 7864336 | tf_op jit(solution)/shard_map/all_gather | solution.py:80
  1174.9 10.7 copy.52
  1185.6 12.1 %fusion.27 = bf16[3,20,8,128]{3,2,1,0:T(8,128)(2,1)S(1)} fusion(bf16[10240,3,128]{0,2,1:T(8,128)(2,1)} %bitcast.127, f32[3,160,10240]{2,1,0:T(8,128)} %get-tuple-element.22, f32[3,160]{1,0:T(4,128)S(1)} %get-tuple-element.13, f32[160,3]{0,1:T(4,128)S(1)} %bitcast.145, f32[160,3]{0,1:T(4,128)S(1)} %get-tuple-element.12), kind=kOutput, calls=%fused_computation.25 | convolution fusion | flops 1273221120 | bytes 27653760 | tf_op jit(solution)/shard_map/hqk,khd->qhd/dot_general | solution.py:92
  (44 shorter events, 7.9 us)
Async XLA Ops:
  7.2 61.4 %copy-start = (bf16[160,384]{1,0:T(8,128)(2,1)S(1)}, bf16[160,384]{1,0:T(8,128)(2,1)}, u32[]{:S(2)}) copy-start(bf16[160,384]{1,0:T(8,128)(2,1)} %param.19) | copy-start | bytes 368644
  9.5 23.7 %all-to-all-start = ((bf16[4,8,384]{2,0,1:T(4,128)(2,1)}), bf16[4,8,384]{2,0,1:T(4,128)(2,1)S(1)}, u32[]{:S(2)}, u32[]{:S(2)}) async-start(bf16[4,8,384]{2,0,1:T(4,128)(2,1)} %bitcast.9), calls=%async_computation | async-start | bytes 49152 | tf_op jit(solution)/shard_map/all_to_all | solution.py:110
  33.2 21.4 %all-to-all-start.1 = ((bf16[4,8,384]{2,0,1:T(4,128)(2,1)}), bf16[4,8,384]{2,0,1:T(4,128)(2,1)S(1)}, u32[]{:S(2)}, u32[]{:S(2)}) async-start(bf16[4,8,384]{2,0,1:T(4,128)(2,1)} %bitcast.146), calls=%async_computation.1 | async-start | bytes 49152 | tf_op jit(solution)/shard_map/all_to_all | solution.py:111
  41.2 188.6 %all-reduce.5.cloned.1.call-start = ((), (), s32[]{:S(2)}) async-start(), calls=%async_computation.6 | async-start | bytes 786432 | tf_op jit(solution)/shard_map/psum | solution.py:146
  72.8 615.6 %all-gather.3.cloned.1.call-start = ((), (), s32[]{:S(2)}) async-start(), calls=%async_computation.4 | async-start | bytes 7987200 | tf_op jit(solution)/shard_map/all_gather | solution.py:79
  75.9 1099.0 %all-gather.5.cloned.1.call-start = ((), (), s32[]{:S(2)}) async-start(), calls=%async_computation.5 | async-start | bytes 7987200 | tf_op jit(solution)/shard_map/all_gather | solution.py:80
  231.2 8.3 all-to-all-start.3
  239.5 8.8 all-to-all-start.2
Sparse Core Ops, SparseCore 0:
  72.9 156.8 all-reduce.4
  232.4 455.9 all-gather.2
  690.5 484.2 all-gather.4
where the time goes:
time: 1210 us
  waiting for transfers between devices  1050 us (87%)
  blocking collectives  37.3 us (3%)
  matrix products  30.6 us (3%)
  local copies, waits for them, and re-layouts  29.3 us (2%)
  starting transfers between devices  27.3 us (2%)
  other arithmetic  18.9 us (2%)
  between operations  13.9 us (1%)
    all_gather x1, waiting for transfers between devices, per_device(): lax.all_gather(self_values, ('row', 'col'), axis=0, tiled=True)  453 us
    all_gather x1, waiting for transfers between devices, per_device(): key_piece = lax.all_gather(key_turned, ('row', 'col'), axis=0, tiled=True)  438 us
    psum x1, waiting for transfers between devices, per_device(): lax.psum((grad_keys, grad_values), ('row', 'col'))  153 us
  transfers between devices with their start and end apart: 7, of which 5 were waited for; matrix products, arithmetic and copies ran while one was open for 4% of the time, Pallas kernels for 0%

commit v1 on v0

v1 whole, which is shorter than its diff:
```python
import functools
import math
import jax
import jax.numpy as jnp
import numpy as np
from jax import lax
from jax.experimental import pallas as pl
from jax.experimental.pallas import tpu as pltpu
from jax.sharding import PartitionSpec as P

D = 128
EPS = 1e-06
MESH = pl.DeviceIdType.MESH
f32 = jnp.float32
bf16 = jnp.bfloat16
NEG = -1e30
NT = (((1,), (1,)), ((), ()))
NN = (((1,), (0,)), ((), ()))
TN = (((0,), (0,)), ((), ()))


def dot(a, b, dims):
    return lax.dot_general(a, b, dims, preferred_element_type=f32)


def freq_rows():
    half = D // 2
    side = D // 6
    time = half - 2 * side
    ft = 1.0 / 10000.0 ** (np.arange(time, dtype=np.float32) * 2.0 / (2 * time))
    fs = 1.0 / 10000.0 ** (np.arange(side, dtype=np.float32) * 2.0 / (2 * side))
    rows = np.zeros((8, half), np.float32)
    rows[0, :time] = ft
    rows[1, time : time + side] = fs
    rows[2, time + side :] = fs
    return np.repeat(rows, 2, axis=1)


def kernel(
    cfg,
    q_ref, k_ref, v_ref, pos_ref, fr_ref, qg_ref, kg_ref, ck_ref, cv_ref, cg_ref, cot_ref,
    so_ref, io_ref, gk_ref, gv_ref,
    Q, K, V, S, O, OR, X1s, X1, X2, ST, MS, MR, LS, LR, G1s, G1, G2s, G2, G3, G4, qp,
    loc_sem, gs_sem, gr_sem, os_sem, or_sem, xs_sem, xr_sem,
):
    E, R, YH, N, T, W, H = cfg
    W2 = W * E
    scale = D ** -0.5
    e = lax.axis_index("enc")
    row = lax.axis_index("row")
    col = lax.axis_index("col")
    z = col // YH
    y = (col % YH) * R + row
    c = e % 2
    a = y * (1 - c) + z * c
    b = z * (1 - c) + y * c
    FW = N // 2
    BW = N - 1 - FW

    def dev(e_, y_, z_):
        return (e_, y_ % R, z_ * YH + y_ // R)

    def e_dev(d):
        return dev((e + d) % E, y, z)

    def y_dev(d):
        return dev(e, (y + d) % N, z)

    def z_dev(d):
        return dev(e, y, (z + d) % N)

    def a_dev(p):
        return dev(e, (1 - c) * p + c * y, (1 - c) * z + c * p)

    def b_dev(p):
        return dev(e, (1 - c) * y + c * p, (1 - c) * p + c * z)

    def row_dev(d):
        return (e, (row + d) % R, col)

    def remote(src, dst, ssem, rsem, device):
        return pltpu.make_async_remote_copy(
            src_ref=src, dst_ref=dst, send_sem=ssem, recv_sem=rsem,
            device_id=device, device_id_type=MESH,
        )

    bar = pltpu.get_barrier_semaphore()
    peers = [e_dev(d) for d in range(1, E)]
    peers += [y_dev(d) for d in range(1, N)] + [z_dev(d) for d in range(1, N)]
    for p in peers:
        pl.semaphore_signal(bar, inc=1, device_id=p, device_id_type=MESH)
    pl.semaphore_wait(bar, len(peers))

    def fwd_pos(p, s):
        return (p + (1 - 2 * c) * s + 2 * N) % N

    def ring(i, buf, p, who, fwd, s):
        sg = 1 if fwd else -1
        slot = fwd_pos(p, -sg * s)
        sl = buf.at[:, pl.ds(pl.multiple_of(slot * T, T), T), :]
        k_ = s if fwd else FW + s
        return remote(sl, sl, gs_sem.at[i, k_], gr_sem.at[i, k_], who(fwd_pos(p, sg)))

    rings = {"q": (0, Q, a, a_dev), "k": (1, K, b, b_dev), "v": (2, V, b, b_dev)}

    def ring_start(t, s):
        if s < FW:
            ring(*rings[t], True, s).start()
        if s < BW:
            ring(*rings[t], False, s).start()

    def ring_recv(t, s):
        if s < FW:
            ring(*rings[t], True, s).wait_recv()
        if s < BW:
            ring(*rings[t], False, s).wait_recv()

    def ring_sent(t):
        for s in range(FW):
            ring(*rings[t], True, s).wait_send()
        for s in range(BW):
            ring(*rings[t], False, s).wait_send()

    def ring_next(t, s):
        ring_recv(t, s - 1)
        if s < FW:
            ring_start(t, s)

    a0 = pl.multiple_of(a * T, T)
    b0 = pl.multiple_of(b * T, T)
    for h in range(H):
        pltpu.make_async_copy(
            v_ref.at[:, pl.ds(h * D, D)], V.at[h, pl.ds(b0, T), :], loc_sem.at[h]
        ).start()

    eye = lax.broadcasted_iota(jnp.int32, (T, T), 0) == lax.broadcasted_iota(jnp.int32, (T, T), 1)

    def to_row(colv):
        return jnp.sum(jnp.where(eye, jnp.broadcast_to(colv, (T, T)), 0.0), axis=0, keepdims=True)

    def to_col(rowv):
        return jnp.sum(jnp.where(eye, jnp.broadcast_to(rowv, (T, T)), 0.0), axis=1, keepdims=True)

    qw = q_ref[...].astype(f32)
    kw = k_ref[...].astype(f32)
    srow_q = to_row(jnp.sum(qw * qw, axis=1, keepdims=True))
    srow_k = to_row(jnp.sum(kw * kw, axis=1, keepdims=True))
    sub8 = lax.broadcasted_iota(jnp.int32, (8, T), 0)
    ST[e] = jnp.where(sub8 < 4, jnp.broadcast_to(srow_q, (8, T)), jnp.broadcast_to(srow_k, (8, T)))

    def xch(i, d, src, dst, device):
        return remote(src, dst, xs_sem.at[i, d], xr_sem.at[i, d], device)

    def st_x(d):
        return xch(0, d, ST.at[e], ST.at[e], e_dev(d))

    for d in range(1, E):
        st_x(d).start()

    for h in range(H):
        pltpu.make_async_copy(
            v_ref.at[:, pl.ds(h * D, D)], V.at[h, pl.ds(b0, T), :], loc_sem.at[h]
        ).wait()
    ring_start("v", 0)

    ckw = ck_ref[...].astype(f32)
    crecip = lax.rsqrt(jnp.mean(ckw * ckw, axis=1, keepdims=True) + EPS)
    cn = (ckw * crecip * cg_ref[...]).astype(bf16).astype(f32)
    cvw = cv_ref[...].astype(f32)
    for j in range(E):
        X1s[j, 0:4, :] = cn[:, j * W : (j + 1) * W]
        X1s[j, 4:8, :] = cvw[:, j * W : (j + 1) * W]

    def x1_x(d):
        return xch(1, d, X1s.at[(e + d) % E], X1.at[e], e_dev(d))

    for d in range(1, E):
        x1_x(d).start()
    X1[e] = X1s[e]

    coords = pos_ref[...].astype(f32)
    ang = (
        coords[:, 0:1] * fr_ref[0:1, :]
        + coords[:, 1:2] * fr_ref[1:2, :]
        + coords[:, 2:3] * fr_ref[2:3, :]
    )
    lane = lax.broadcasted_iota(jnp.int32, (T, D), 1)
    even = lane % 2 == 0
    cosv = jnp.cos(ang)
    sinv = jnp.sin(ang)
    sinv = jnp.where(even, -sinv, sinv)

    for d in range(1, E):
        st_x(d).wait_recv()
    tot = ST[0]
    for j in range(1, E):
        tot = tot + ST[j]
    qn = qw * lax.rsqrt(to_col(tot[0:1, :]) / W2 + EPS) * qg_ref[...]
    kn = kw * lax.rsqrt(to_col(tot[4:5, :]) / W2 + EPS) * kg_ref[...]
    qp[...] = qn.astype(bf16)

    def turn(x):
        swapped = jnp.where(even, pltpu.roll(x, D - 1, 1), pltpu.roll(x, 1, 1))
        return (x * cosv + swapped * sinv).astype(bf16)

    for h in range(H):
        Q[h, pl.ds(a0, T), :] = turn(qn[:, h * D : (h + 1) * D])
        K[h, pl.ds(b0, T), :] = turn(kn[:, h * D : (h + 1) * D])
    ring_start("q", 0)
    ring_start("k", 0)

    for d in range(1, E):
        x1_x(d).wait_recv()
    X2[row] = X1[...].reshape(E * 8, W).astype(bf16)

    def x2_x(d):
        return xch(2, d, X2.at[row], X2.at[row], row_dev(d))

    for d in range(1, R):
        x2_x(d).start()
    ring_next("v", 1)
    ring_next("q", 1)
    ring_next("k", 1)
    for d in range(1, R):
        x2_x(d).wait_recv()

    C2 = R * E * 8
    xall = X2[...].reshape(C2, W)
    xval = pltpu.roll(xall.astype(f32), C2 - 4, 0).astype(bf16)
    is_key_l = lax.broadcasted_iota(jnp.int32, (T, C2), 1) % 8 < 4
    is_key_s = lax.broadcasted_iota(jnp.int32, (C2, D), 0) % 8 < 4

    def image_head(h):
        hs = slice(h * D, (h + 1) * D)
        qh = qp[:, hs]
        th = cot_ref[:, hs]
        sc = dot(qh, xall[:, hs], NT) * scale
        sc = jnp.where(is_key_l, sc, NEG)
        w = jnp.exp(sc - jnp.max(sc, axis=1, keepdims=True))
        pr = w / jnp.sum(w, axis=1, keepdims=True)
        plo = pr.astype(bf16)
        io_ref[:, hs] = dot(plo, xval[:, hs], NN).astype(bf16)
        gv = dot(plo, th, TN)
        gp = dot(th, xval[:, hs], NT)
        inner = jnp.sum(pr * gp, axis=1, keepdims=True)
        gsc = (pr * (gp - inner)).astype(bf16)
        gk = dot(gsc, qh, TN) * scale
        both = jnp.where(is_key_s, gk, pltpu.roll(gv, 4, 0))
        for r in range(R):
            for j in range(E):
                lo = (r * E + j) * 8
                G1s[j, r, :, hs] = both[lo : lo + 8, :]

    for s in range(2, FW + 1):
        if s - 2 < H:
            image_head(s - 2)
        for t in ("v", "q", "k"):
            ring_next(t, s)
    for h in range(FW - 1, H):
        image_head(h)

    def g1_x(d):
        j = (z + d) % N
        return xch(3, d, G1s.at[j], G1.at[z], z_dev(d))

    for d in range(1, N):
        g1_x(d).start()
    G1[z] = G1s[z]

    def pass1(h):
        def body(i, carry):
            rows = pl.ds(pl.multiple_of(i * T, T), T)
            s = dot(Q[h, rows, :], K[h], NT)
            S[h, rows, :] = s
            MS[h, pl.ds(i, 1), :] = to_row(jnp.max(s, axis=1, keepdims=True))
            return carry

        lax.fori_loop(0, N, body, 0)

    def m_x(h, d):
        return xch(6 + h, d, MS.at[h], MR.at[h, a], a_dev((a + d) % N))

    def send_max(h):
        for d in range(1, N):
            m_x(h, d).start()
        MR[h, a] = MS[h]

    for h in range(H):
        pass1(h)
        send_max(h)
        if h == min(1, H - 1):
            for d in range(1, N):
                g1_x(d).wait_recv()
            g = G1[0]
            for j in range(1, N):
                g = g + G1[j]
            G2s[...] = g

            def g2_x(d):
                return xch(4, d, G2s.at[(y + d) % N % R], G2.at[y], y_dev(d))

            for d in range(1, N):
                g2_x(d).start()
            G2[y] = G2s[row]

    def pass2(h):
        for d in range(1, N):
            m_x(h, d).wait_recv()
        gm = MR[h, 0]
        for j in range(1, N):
            gm = jnp.maximum(gm, MR[h, j])
        MS[H] = gm

        def body(i, carry):
            rows = pl.ds(pl.multiple_of(i * T, T), T)
            mc = to_col(MS[H, pl.ds(i, 1), :])
            w = jnp.exp2((S[h, rows, :] - mc) * (scale * math.log2(math.e)))
            LS[i, h : h + 1, :] = to_row(jnp.sum(w, axis=1, keepdims=True))
            O[h, i] = dot(w.astype(bf16), V[h], NN)
            return carry

        lax.fori_loop(0, N, body, 0)

    def o_x(h, d):
        p = (a + d) % N
        return remote(
            O.at[h, p], OR.at[h, d], os_sem.at[h, d], or_sem.at[h, d], a_dev(p)
        )

    def l_x(d):
        p = (a + d) % N
        return xch(5, d, LS.at[p], LR.at[a], a_dev(p))

    for h in range(H):
        pass2(h)
        for d in range(1, N):
            o_x(h, d).start()
        if h == 0:
            for d in range(1, N):
                g2_x(d).wait_recv()
            g = G2[0]
            for j in range(1, N):
                g = g + G2[j]
            G3[z] = g

            def g3_x(d):
                return xch(6 + H, d, G3.at[z], G3.at[z], z_dev(d))

            for d in range(1, N):
                g3_x(d).start()
    for d in range(1, N):
        l_x(d).start()
    LR[a] = LS[a]

    for d in range(1, N):
        g3_x(d).wait_recv()

    def g4_x(d):
        return xch(7 + H, d, G3.at[(e + d) % E], G4.at[e], e_dev(d))

    for d in range(1, E):
        g4_x(d).start()
    G4[e] = G3[e]

    for d in range(1, N):
        l_x(d).wait_recv()
    lt = LR[0]
    for j in range(1, N):
        lt = lt + LR[j]

    for d in range(1, E):
        g4_x(d).wait_recv()
    for j in range(E):
        js = slice(j * W, (j + 1) * W)
        gv_ref[:, js] = G4[j, 4:8, :]
        gk_ref[:, js] = G4[j, 0:4, :]
    sg = cg_ref[...] * gk_ref[...]
    gk_ref[...] = crecip * sg - ckw * (crecip * crecip * crecip) * jnp.mean(
        ckw * sg, axis=1, keepdims=True
    )

    for h in range(H):
        acc = O[h, a]
        for d in range(1, N):
            o_x(h, d).wait_recv()
            acc = acc + OR[h, d]
        so_ref[:, h * D : (h + 1) * D] = (acc / to_col(lt[h : h + 1, :])).astype(bf16)

    for t in ("q", "k", "v"):
        ring_sent(t)
    for d in range(1, E):
        st_x(d).wait_send()
        x1_x(d).wait_send()
        g4_x(d).wait_send()
    for d in range(1, R):
        x2_x(d).wait_send()
    for d in range(1, N):
        g1_x(d).wait_send()
        g2_x(d).wait_send()
        g3_x(d).wait_send()
        l_x(d).wait_send()
        for h in range(H):
            m_x(h, d).wait_send()
            o_x(h, d).wait_send()


def per_device(mesh_shape, q, k, v, pos, qg, kg, ck, cv, cg, cot):
    E, R, CL = mesh_shape
    T, W = q.shape
    H = W // D
    N = int(math.isqrt(R * CL))
    YH = N // R
    cfg = (E, R, YH, N, T, W, H)
    vm = pl.BlockSpec(memory_space=pltpu.VMEM)
    dma = pltpu.SemaphoreType.DMA
    out_shape = (
        jax.ShapeDtypeStruct((T, W), bf16),
        jax.ShapeDtypeStruct((T, W), bf16),
        jax.ShapeDtypeStruct(ck.shape, f32),
        jax.ShapeDtypeStruct(ck.shape, f32),
    )
    MX = max(E, N)
    scratch = [
        pltpu.VMEM((H, N * T, D), bf16),
        pltpu.VMEM((H, N * T, D), bf16),
        pltpu.VMEM((H, N * T, D), bf16),
        pltpu.VMEM((H, N * T, N * T), f32),
        pltpu.VMEM((H, N, T, D), f32),
        pltpu.VMEM((H, N, T, D), f32),
        pltpu.VMEM((E, 8, W), f32),
        pltpu.VMEM((E, 8, W), f32),
        pltpu.VMEM((R, E * 8, W), bf16),
        pltpu.VMEM((E, 8, T), f32),
        pltpu.VMEM((H + 1, N, T), f32),
        pltpu.VMEM((H, N, N, T), f32),
        pltpu.VMEM((N, 8, T), f32),
        pltpu.VMEM((N, 8, T), f32),
        pltpu.VMEM((N, R, 8, W), f32),
        pltpu.VMEM((N, R, 8, W), f32),
        pltpu.VMEM((R, 8, W), f32),
        pltpu.VMEM((N, 8, W), f32),
        pltpu.VMEM((N, 8, W), f32),
        pltpu.VMEM((E, 8, W), f32),
        pltpu.VMEM((T, W), bf16),
        dma((H,)),
        dma((3, N)),
        dma((3, N)),
        dma((H, N)),
        dma((H, N)),
        dma((8 + H, MX)),
        dma((8 + H, MX)),
    ]
    return pl.pallas_call(
        functools.partial(kernel, cfg),
        out_shape=out_shape,
        in_specs=[vm] * 11,
        out_specs=(vm,) * 4,
        scratch_shapes=scratch,
        compiler_params=pltpu.CompilerParams(
            collective_id=0, has_side_effects=True, vmem_limit_bytes=56 * 2**20
        ),
    )(q, k, v, pos, jnp.asarray(freq_rows()), qg[None, :], kg[None, :], ck, cv, cg[None, :], cot)


def solution(mesh):
    shape = (mesh.shape["enc"], mesh.shape["row"], mesh.shape["col"])
    tok = P(("row", "col"), "enc")
    ctx = P(("enc", "row"), None)
    return jax.shard_map(
        functools.partial(per_device, shape),
        mesh=mesh,
        in_specs=(tok, tok, tok, P(("row", "col"), None), P("enc"), P("enc"), ctx, ctx, P(), tok),
        out_specs=(tok, tok, ctx, ctx),
        check_vma=False,
    )
```

time: 1210 us -> 96.2 us (0.08)
  the two profiles are of different devices: /device:TPU:6 before, /device:TPU:1 now
where the time goes in v1:
time: 96.2 us; the launch traced here: 95.9 us
  Pallas kernels  88.1 us (92%)
  local copies, waits for them, and re-layouts  7.09 us (7%)
    pallas_call x1, Pallas kernels, per_device(): pl.pallas_call(functools.partial(kernel, cfg), out_shape=out_shape, in_sp...  88.1 us
    unnamed x13, local copies, waits for them, and re-layouts  4.59 us

profile of v1, /device:TPU:1, one launch (start us, length us, event | category | flops | bytes accessed | tf_op | source)
XLA Modules:
  0.0 95.9 jit_solution(10602891511502419865)
XLA Ops:
  0.6 0.0 copy-start.3
  0.6 1.3 %broadcast_in_dim.9.qg_ref = f32[1,384]{1,0:T(1,128)} reshape(f32[384]{0:T(512)} %param.15) | data formatting | bytes 3072 | tf_op jit(solution)/shard_map/broadcast_in_dim | solution.py:462
  1.9 1.2 %broadcast_in_dim.10.kg_ref = f32[1,384]{1,0:T(1,128)} reshape(f32[384]{0:T(512)} %param.16) | data formatting | bytes 3072 | tf_op jit(solution)/shard_map/broadcast_in_dim | solution.py:462
  3.1 0.0 copy-done.3
  3.1 0.8 copy.15.pos_ref
  3.9 88.1 %shard_map.138 = (bf16[160,384]{1,0:T(8,128)(2,1)}, bf16[160,384]{1,0:T(8,128)(2,1)}, f32[4,3072]{1,0:T(4,128)}, f32[4,3072]{1,0:T(4,128)}) custom-call(bf16[160,384]{1,0:T(8,128)(2,1)} %q_ref.1, bf16[160,384]{1,0:T(8,128)(2,1)} %k_ref.1, bf16[160,384]{1,0:T(8,128)(2,1)} %v_ref.1, s32[160,3]{1,0:T(8,128)} %copy.15.pos_ref, f32[8,128]{1,0:T(8,128)} %constant.2.clone.fr_ref, ...), custom_call_target="tpu_custom_call" | custom-call | tf_op jit(solution)/shard_map/pallas_call | solution.py:453
  92.0 0.0 copy-start
  92.0 1.6 %copy.20 = bf16[160,384]{1,0:T(8,128)(2,1)} copy(bf16[160,384]{1,0:T(8,128)(2,1)} %get-tuple-element.8) | data formatting | bytes 245760
  93.6 0.0 copy-done
  93.6 0.0 copy-start.2
  93.6 0.6 copy.21
  94.3 0.1 copy-done.2
  94.4 0.0 copy-start.1
  94.4 0.6 copy.22
  95.1 0.2 copy-done.1
  95.2 0.6 copy.23
Async XLA Ops:
  0.6 2.5 %copy-start.3 = (s32[160,3]{0,1:T(4,128)S(1)}, s32[160,3]{0,1:T(4,128)}, u32[]{:S(2)}) copy-start(s32[160,3]{0,1:T(4,128)} %param.14) | copy-start | bytes 5764
  92.0 1.6 %copy-start = (bf16[160,384]{1,0:T(8,128)(2,1)S(1)}, bf16[160,384]{1,0:T(8,128)(2,1)}, u32[]{:S(2)}) copy-start(bf16[160,384]{1,0:T(8,128)(2,1)} %get-tuple-element.9) | copy-start | bytes 368644
  93.6 0.8 copy-start.2
  94.4 0.8 copy-start.1

commit v2 on v1

--- a/solution.py
+++ b/solution.py
@@ -40,7 +40,7 @@
     cfg,
     q_ref, k_ref, v_ref, pos_ref, fr_ref, qg_ref, kg_ref, ck_ref, cv_ref, cg_ref, cot_ref,
     so_ref, io_ref, gk_ref, gv_ref,
-    Q, K, V, S, O, OR, X1s, X1, X2, ST, MS, MR, LS, LR, G1s, G1, G2s, G2, G3, G4, qp,
+    Q, K, V, S, O, ORF, ORB, X1s, X1, X2, ST, MS, MR, LS, LR, G1s, G1, G2s, G2, G3, G4, qp,
     loc_sem, gs_sem, gr_sem, os_sem, or_sem, xs_sem, xr_sem,
 ):
     E, R, YH, N, T, W, H = cfg
@@ -87,44 +87,56 @@
     bar = pltpu.get_barrier_semaphore()
     peers = [e_dev(d) for d in range(1, E)]
     peers += [y_dev(d) for d in range(1, N)] + [z_dev(d) for d in range(1, N)]
+    peers += [dev(z, y, (z + d) % N) for d in range(1, N)]
+    peers += [dev((e + d) % E, y, e) for d in range(1, E)]
     for p in peers:
         pl.semaphore_signal(bar, inc=1, device_id=p, device_id_type=MESH)
-    pl.semaphore_wait(bar, len(peers))
+
+    @pl.when(e != z)
+    def _():
+        for p in (dev(z, y, z), dev(e, y, e)):
+            pl.semaphore_signal(bar, inc=1, device_id=p, device_id_type=MESH)
+
+    BAR = len(peers) + jnp.where(e != z, 2, 0)
 
     def fwd_pos(p, s):
         return (p + (1 - 2 * c) * s + 2 * N) % N
 
-    def ring(i, buf, p, who, fwd, s):
+    def ring(i, buf, p, who, h, fwd, s):
         sg = 1 if fwd else -1
-        slot = fwd_pos(p, -sg * s)
-        sl = buf.at[:, pl.ds(pl.multiple_of(slot * T, T), T), :]
+        rows = pl.ds(pl.multiple_of(fwd_pos(p, -sg * s) * T, T), T)
+        sl = buf.at[:, rows, :] if h is None else buf.at[h, rows, :]
         k_ = s if fwd else FW + s
-        return remote(sl, sl, gs_sem.at[i, k_], gr_sem.at[i, k_], who(fwd_pos(p, sg)))
+        g = 0 if h is None else h
+        return remote(
+            sl, sl, gs_sem.at[i, g, k_], gr_sem.at[i, g, k_], who(fwd_pos(p, sg))
+        )
 
     rings = {"q": (0, Q, a, a_dev), "k": (1, K, b, b_dev), "v": (2, V, b, b_dev)}
 
-    def ring_start(t, s):
+    def ring_start(t, h, s):
         if s < FW:
-            ring(*rings[t], True, s).start()
+            ring(*rings[t], h, True, s).start()
         if s < BW:
-            ring(*rings[t], False, s).start()
-
-    def ring_recv(t, s):
+            ring(*rings[t], h, False, s).start()
+
+    def ring_recv(t, h, s):
         if s < FW:
-            ring(*rings[t], True, s).wait_recv()
+            ring(*rings[t], h, True, s).wait_recv()
         if s < BW:
-            ring(*rings[t], False, s).wait_recv()
-
-    def ring_sent(t):
+            ring(*rings[t], h, False, s).wait_recv()
+
+    def ring_sent(t, h):
         for s in range(FW):
-            ring(*rings[t], True, s).wait_send()
+            ring(*rings[t], h, True, s).wait_send()
         for s in range(BW):
-            ring(*rings[t], False, s).wait_send()
-
-    def ring_next(t, s):
-        ring_recv(t, s - 1)
-        if s < FW:
-            ring_start(t, s)
+            ring(*rings[t], h, False, s).wait_send()
+
+    def ring_next(t, h, s):
+        if s >= FW:
+            return
+        ring_recv(t, h, s - 1)
+        ring_start(t, h, s)
 
     a0 = pl.multiple_of(a * T, T)
     b0 = pl.multiple_of(b * T, T)
@@ -154,6 +166,7 @@
     def st_x(d):
         return xch(0, d, ST.at[e], ST.at[e], e_dev(d))
 
+    pl.semaphore_wait(bar, BAR)
     for d in range(1, E):
         st_x(d).start()
 
@@ -161,11 +174,11 @@
         pltpu.make_async_copy(
             v_ref.at[:, pl.ds(h * D, D)], V.at[h, pl.ds(b0, T), :], loc_sem.at[h]
         ).wait()
-    ring_start("v", 0)
+    ring_start("v", None, 0)
 
     ckw = ck_ref[...].astype(f32)
     crecip = lax.rsqrt(jnp.mean(ckw * ckw, axis=1, keepdims=True) + EPS)
-    cn = (ckw * crecip * cg_ref[...]).astype(bf16).astype(f32)
+    cn = (ckw * crecip * cg_ref[...].reshape(1, W2)).astype(bf16).astype(f32)
     cvw = cv_ref[...].astype(f32)
     for j in range(E):
         X1s[j, 0:4, :] = cn[:, j * W : (j + 1) * W]
@@ -180,9 +193,9 @@
 
     coords = pos_ref[...].astype(f32)
     ang = (
-        coords[:, 0:1] * fr_ref[0:1, :]
-        + coords[:, 1:2] * fr_ref[1:2, :]
-        + coords[:, 2:3] * fr_ref[2:3, :]
+        to_col(coords[0:1, :]) * fr_ref[0:1, :]
+        + to_col(coords[1:2, :]) * fr_ref[1:2, :]
+        + to_col(coords[2:3, :]) * fr_ref[2:3, :]
     )
     lane = lax.broadcasted_iota(jnp.int32, (T, D), 1)
     even = lane % 2 == 0
@@ -190,13 +203,14 @@
     sinv = jnp.sin(ang)
     sinv = jnp.where(even, -sinv, sinv)
 
+    ring_next("v", None, 1)
     for d in range(1, E):
         st_x(d).wait_recv()
     tot = ST[0]
     for j in range(1, E):
         tot = tot + ST[j]
-    qn = qw * lax.rsqrt(to_col(tot[0:1, :]) / W2 + EPS) * qg_ref[...]
-    kn = kw * lax.rsqrt(to_col(tot[4:5, :]) / W2 + EPS) * kg_ref[...]
+    qn = qw * lax.rsqrt(to_col(tot[0:1, :]) / W2 + EPS) * qg_ref[...].reshape(1, W)
+    kn = kw * lax.rsqrt(to_col(tot[4:5, :]) / W2 + EPS) * kg_ref[...].reshape(1, W)
     qp[...] = qn.astype(bf16)
 
     def turn(x):
@@ -205,23 +219,30 @@
 
     for h in range(H):
         Q[h, pl.ds(a0, T), :] = turn(qn[:, h * D : (h + 1) * D])
+        ring_start("q", h, 0)
         K[h, pl.ds(b0, T), :] = turn(kn[:, h * D : (h + 1) * D])
-    ring_start("q", 0)
-    ring_start("k", 0)
+        ring_start("k", h, 0)
+    ring_next("v", None, 2)
 
     for d in range(1, E):
         x1_x(d).wait_recv()
     X2[row] = X1[...].reshape(E * 8, W).astype(bf16)
 
+    sig = 1 - 2 * c
+    offs = {1: [], 2: [1], 4: [1, -1, 2 * sig]}[R]
+
     def x2_x(d):
-        return xch(2, d, X2.at[row], X2.at[row], row_dev(d))
-
-    for d in range(1, R):
+        return xch(2, d, X2.at[row], X2.at[row], y_dev(offs[d] + N))
+
+    for d in range(len(offs)):
         x2_x(d).start()
-    ring_next("v", 1)
-    ring_next("q", 1)
-    ring_next("k", 1)
-    for d in range(1, R):
+    for s in range(1, FW):
+        for h in range(H):
+            ring_next("q", h, s)
+            ring_next("k", h, s)
+        if s + 2 < FW:
+            ring_next("v", None, s + 2)
+    for d in range(len(offs)):
         x2_x(d).wait_recv()
 
     C2 = R * E * 8
@@ -251,12 +272,7 @@
                 lo = (r * E + j) * 8
                 G1s[j, r, :, hs] = both[lo : lo + 8, :]
 
-    for s in range(2, FW + 1):
-        if s - 2 < H:
-            image_head(s - 2)
-        for t in ("v", "q", "k"):
-            ring_next(t, s)
-    for h in range(FW - 1, H):
+    for h in range(H):
         image_head(h)
 
     def g1_x(d):
@@ -286,22 +302,35 @@
         MR[h, a] = MS[h]
 
     for h in range(H):
+        ring_recv("q", h, FW - 1)
+        ring_recv("k", h, FW - 1)
         pass1(h)
         send_max(h)
-        if h == min(1, H - 1):
-            for d in range(1, N):
-                g1_x(d).wait_recv()
-            g = G1[0]
-            for j in range(1, N):
-                g = g + G1[j]
-            G2s[...] = g
-
-            def g2_x(d):
-                return xch(4, d, G2s.at[(y + d) % N % R], G2.at[y], y_dev(d))
-
-            for d in range(1, N):
-                g2_x(d).start()
-            G2[y] = G2s[row]
+
+    def of(h, s):
+        t = fwd_pos(a, FW - s)
+        return remote(
+            O.at[h, t], ORF.at[h, s], os_sem.at[h, s], or_sem.at[h, s], a_dev(fwd_pos(a, 1))
+        ), t
+
+    def ob(h, s):
+        t = fwd_pos(a, s - BW)
+        return remote(
+            O.at[h, t], ORB.at[h, s], os_sem.at[h, FW + s], or_sem.at[h, FW + s],
+            a_dev(fwd_pos(a, -1)),
+        ), t
+
+    def o_step(h, s):
+        if s < FW:
+            of(h, s - 1)[0].wait_recv()
+            cp, t = of(h, s)
+            O[h, t] = O[h, t] + ORF[h, s - 1]
+            cp.start()
+        if s < BW:
+            ob(h, s - 1)[0].wait_recv()
+            cp, t = ob(h, s)
+            O[h, t] = O[h, t] + ORB[h, s - 1]
+            cp.start()
 
     def pass2(h):
         for d in range(1, N):
@@ -311,7 +340,8 @@
             gm = jnp.maximum(gm, MR[h, j])
         MS[H] = gm
 
-        def body(i, carry):
+        def body(k_, carry):
+            i = fwd_pos(a, (2 * (k_ % 2) - 1) * (FW - (k_ + 1) // 2))
             rows = pl.ds(pl.multiple_of(i * T, T), T)
             mc = to_col(MS[H, pl.ds(i, 1), :])
             w = jnp.exp2((S[h, rows, :] - mc) * (scale * math.log2(math.e)))
@@ -319,81 +349,117 @@
             O[h, i] = dot(w.astype(bf16), V[h], NN)
             return carry
 
-        lax.fori_loop(0, N, body, 0)
-
-    def o_x(h, d):
-        p = (a + d) % N
-        return remote(
-            O.at[h, p], OR.at[h, d], os_sem.at[h, d], or_sem.at[h, d], a_dev(p)
-        )
+        body(0, 0)
+        of(h, 0)[0].start()
+        lax.fori_loop(1, 3, body, 0)
+        ob(h, 0)[0].start()
+        lax.fori_loop(3, N, body, 0)
 
     def l_x(d):
         p = (a + d) % N
         return xch(5, d, LS.at[p], LR.at[a], a_dev(p))
 
+    def g2_x(d):
+        return xch(4, d, G2s.at[(y + d) % N % R], G2.at[y], y_dev(d))
+
+    def g3_x(d):
+        i = 6 + H
+        return remote(
+            G3.at[0], G4.at[e], xs_sem.at[i, d], xr_sem.at[i, e], dev(z, y, (z + d) % N)
+        )
+
+    def g3_from(d):
+        i, j = 6 + H, (e + d) % E
+        return remote(G3.at[0], G4.at[j], xs_sem.at[i, d], xr_sem.at[i, j], dev(j, y, e))
+
+    ring_recv("v", None, FW - 1)
     for h in range(H):
         pass2(h)
-        for d in range(1, N):
-            o_x(h, d).start()
+        for j in range(h, -1, -1):
+            o_step(j, h - j + 1)
         if h == 0:
             for d in range(1, N):
-                g2_x(d).wait_recv()
-            g = G2[0]
+                g1_x(d).wait_recv()
+            g = G1[0]
             for j in range(1, N):
-                g = g + G2[j]
-            G3[z] = g
-
-            def g3_x(d):
-                return xch(6 + H, d, G3.at[z], G3.at[z], z_dev(d))
-
+                g = g + G1[j]
+            G2s[...] = g
             for d in range(1, N):
-                g3_x(d).start()
+                g2_x(d).start()
+            G2[y] = G2s[row]
     for d in range(1, N):
         l_x(d).start()
     LR[a] = LS[a]
 
     for d in range(1, N):
-        g3_x(d).wait_recv()
-
-    def g4_x(d):
-        return xch(7 + H, d, G3.at[(e + d) % E], G4.at[e], e_dev(d))
-
-    for d in range(1, E):
-        g4_x(d).start()
-    G4[e] = G3[e]
+        g2_x(d).wait_recv()
+    g = G2[0]
+    for j in range(1, N):
+        g = g + G2[j]
+    G3[0] = g
+
+    @pl.when(e != z)
+    def _():
+        g3_x(0).start()
+
+    @pl.when(e == z)
+    def _():
+        G4[e] = g
+
+    for d in range(1, N):
+        g3_x(d).start()
+
+    lt = None
+    for k_ in range(H, H + FW):
+        for j in range(H - 1, -1, -1):
+            s_ = k_ - j
+            if 1 <= s_ < FW and s_ >= H - j + 1 - 0:
+                o_step(j, s_)
 
     for d in range(1, N):
         l_x(d).wait_recv()
     lt = LR[0]
     for j in range(1, N):
         lt = lt + LR[j]
+    for h in range(H):
+        of(h, FW - 1)[0].wait_recv()
+        ob(h, BW - 1)[0].wait_recv()
+        acc = O[h, a] + ORF[h, FW - 1] + ORB[h, BW - 1]
+        so_ref[:, h * D : (h + 1) * D] = (acc / to_col(lt[h : h + 1, :])).astype(bf16)
+
+    @pl.when(e != z)
+    def _():
+        g3_from(0).wait_recv()
 
     for d in range(1, E):
-        g4_x(d).wait_recv()
+        g3_from(d).wait_recv()
     for j in range(E):
         js = slice(j * W, (j + 1) * W)
         gv_ref[:, js] = G4[j, 4:8, :]
         gk_ref[:, js] = G4[j, 0:4, :]
-    sg = cg_ref[...] * gk_ref[...]
+    sg = cg_ref[...].reshape(1, W2) * gk_ref[...]
     gk_ref[...] = crecip * sg - ckw * (crecip * crecip * crecip) * jnp.mean(
         ckw * sg, axis=1, keepdims=True
     )
 
     for h in range(H):
-        acc = O[h, a]
-        for d in range(1, N):
-            o_x(h, d).wait_recv()
-            acc = acc + OR[h, d]
-        so_ref[:, h * D : (h + 1) * D] = (acc / to_col(lt[h : h + 1, :])).astype(bf16)
-
-    for t in ("q", "k", "v"):
-        ring_sent(t)
+        ring_sent("q", h)
+        ring_sent("k", h)
+        for s in range(FW):
+            of(h, s)[0].wait_send()
+        for s in range(BW):
+            ob(h, s)[0].wait_send()
+    ring_sent("v", None)
     for d in range(1, E):
         st_x(d).wait_send()
         x1_x(d).wait_send()
-        g4_x(d).wait_send()
-    for d in range(1, R):
+    for d in range(len(offs)):
         x2_x(d).wait_send()
+
+    @pl.when(e != z)
+    def _():
+        g3_x(0).wait_send()
+
     for d in range(1, N):
         g1_x(d).wait_send()
         g2_x(d).wait_send()
@@ -401,7 +467,6 @@
         l_x(d).wait_send()
         for h in range(H):
             m_x(h, d).wait_send()
-            o_x(h, d).wait_send()
 
 
 def per_device(mesh_shape, q, k, v, pos, qg, kg, ck, cv, cg, cot):
@@ -426,7 +491,8 @@
         pltpu.VMEM((H, N * T, D), bf16),
         pltpu.VMEM((H, N * T, N * T), f32),
         pltpu.VMEM((H, N, T, D), f32),
-        pltpu.VMEM((H, N, T, D), f32),
+        pltpu.VMEM((H, N // 2, T, D), f32),
+        pltpu.VMEM((H, N // 2, T, D), f32),
         pltpu.VMEM((E, 8, W), f32),
         pltpu.VMEM((E, 8, W), f32),
         pltpu.VMEM((R, E * 8, W), bf16),
@@ -443,8 +509,8 @@
         pltpu.VMEM((E, 8, W), f32),
         pltpu.VMEM((T, W), bf16),
         dma((H,)),
-        dma((3, N)),
-        dma((3, N)),
+        dma((3, H, N)),
+        dma((3, H, N)),
         dma((H, N)),
         dma((H, N)),
         dma((8 + H, MX)),
@@ -459,7 +525,7 @@
         compiler_params=pltpu.CompilerParams(
             collective_id=0, has_side_effects=True, vmem_limit_bytes=56 * 2**20
         ),
-    )(q, k, v, pos, jnp.asarray(freq_rows()), qg[None, :], kg[None, :], ck, cv, cg[None, :], cot)
+    )(q, k, v, pos.T, jnp.asarray(freq_rows()), qg, kg, ck, cv, cg, cot)
 
 
 def solution(mesh):

time: 96.2 us -> 83.5 us (0.87)
  the two profiles are of different devices: /device:TPU:1 before, /device:TPU:6 now
where the time goes in v2:
time: 83.5 us; the launch traced here: 82.4 us
  Pallas kernels  77.9 us (93%)
  local copies, waits for them, and re-layouts  3.83 us (5%)
    pallas_call x1, Pallas kernels, per_device(): pl.pallas_call(functools.partial(kernel, cfg), out_shape=out_shape, in_sp...  77.9 us
    unnamed x10, local copies, waits for them, and re-layouts  3.83 us

profile of v2, /device:TPU:6, one launch (start us, length us, event | category | flops | bytes accessed | tf_op | source)
XLA Modules:
  0.0 82.4 jit_solution(5968239935091802885)
XLA Ops:
  0.6 77.9 %shard_map.138 = (bf16[160,384]{1,0:T(8,128)(2,1)}, bf16[160,384]{1,0:T(8,128)(2,1)}, f32[4,3072]{1,0:T(4,128)}, f32[4,3072]{1,0:T(4,128)}) custom-call(bf16[160,384]{1,0:T(8,128)(2,1)} %q_ref.1, bf16[160,384]{1,0:T(8,128)(2,1)} %k_ref.1, bf16[160,384]{1,0:T(8,128)(2,1)} %v_ref.1, s32[3,160]{1,0:T(4,128)} %bitcast.1, f32[8,128]{1,0:T(8,128)} %constant.2.clone.fr_ref, ...), custom_call_target="tpu_custom_call" | custom-call | tf_op jit(solution)/shard_map/pallas_call | solution.py:519
  78.6 0.0 copy-start
  78.6 1.6 %copy.19 = bf16[160,384]{1,0:T(8,128)(2,1)} copy(bf16[160,384]{1,0:T(8,128)(2,1)} %get-tuple-element.8) | data formatting | bytes 245760
  80.2 0.0 copy-done
  80.2 0.0 copy-start.2
  80.2 0.6 copy.20
  80.8 0.1 copy-done.2
  81.0 0.0 copy-start.1
  81.0 0.6 copy.21
  81.6 0.2 copy-done.1
  81.8 0.6 copy.22
Async XLA Ops:
  78.6 1.6 %copy-start = (bf16[160,384]{1,0:T(8,128)(2,1)S(1)}, bf16[160,384]{1,0:T(8,128)(2,1)}, u32[]{:S(2)}) copy-start(bf16[160,384]{1,0:T(8,128)(2,1)} %get-tuple-element.9) | copy-start | bytes 368644
  80.2 0.8 copy-start.2
  81.0 0.8 copy-start.1

commit v3 on v2

--- a/solution.py
+++ b/solution.py
@@ -87,17 +87,10 @@
     bar = pltpu.get_barrier_semaphore()
     peers = [e_dev(d) for d in range(1, E)]
     peers += [y_dev(d) for d in range(1, N)] + [z_dev(d) for d in range(1, N)]
-    peers += [dev(z, y, (z + d) % N) for d in range(1, N)]
-    peers += [dev((e + d) % E, y, e) for d in range(1, E)]
     for p in peers:
         pl.semaphore_signal(bar, inc=1, device_id=p, device_id_type=MESH)
 
-    @pl.when(e != z)
-    def _():
-        for p in (dev(z, y, z), dev(e, y, e)):
-            pl.semaphore_signal(bar, inc=1, device_id=p, device_id_type=MESH)
-
-    BAR = len(peers) + jnp.where(e != z, 2, 0)
+    BAR = len(peers)
 
     def fwd_pos(p, s):
         return (p + (1 - 2 * c) * s + 2 * N) % N
@@ -222,7 +215,6 @@
         ring_start("q", h, 0)
         K[h, pl.ds(b0, T), :] = turn(kn[:, h * D : (h + 1) * D])
         ring_start("k", h, 0)
-    ring_next("v", None, 2)
 
     for d in range(1, E):
         x1_x(d).wait_recv()
@@ -240,8 +232,6 @@
         for h in range(H):
             ring_next("q", h, s)
             ring_next("k", h, s)
-        if s + 2 < FW:
-            ring_next("v", None, s + 2)
     for d in range(len(offs)):
         x2_x(d).wait_recv()
 
@@ -274,6 +264,7 @@
 
     for h in range(H):
         image_head(h)
+    ring_next("v", None, 2)
 
     def g1_x(d):
         j = (z + d) % N
@@ -285,13 +276,15 @@
 
     def pass1(h):
         def body(i, carry):
-            rows = pl.ds(pl.multiple_of(i * T, T), T)
+            rows = pl.ds(pl.multiple_of(i * 2 * T, 2 * T), 2 * T)
             s = dot(Q[h, rows, :], K[h], NT)
             S[h, rows, :] = s
-            MS[h, pl.ds(i, 1), :] = to_row(jnp.max(s, axis=1, keepdims=True))
+            m = jnp.max(s, axis=1, keepdims=True)
+            MS[h, pl.ds(2 * i, 1), :] = to_row(m[:T])
+            MS[h, pl.ds(2 * i + 1, 1), :] = to_row(m[T:])
             return carry
 
-        lax.fori_loop(0, N, body, 0)
+        lax.fori_loop(0, N // 2, body, 0)
 
     def m_x(h, d):
         return xch(6 + h, d, MS.at[h], MR.at[h, a], a_dev((a + d) % N))
@@ -306,6 +299,8 @@
         ring_recv("k", h, FW - 1)
         pass1(h)
         send_max(h)
+        if h == 0:
+            ring_next("v", None, 3)
 
     def of(h, s):
         t = fwd_pos(a, FW - s)
@@ -340,20 +335,27 @@
             gm = jnp.maximum(gm, MR[h, j])
         MS[H] = gm
 
-        def body(k_, carry):
+        def weights(k_):
             i = fwd_pos(a, (2 * (k_ % 2) - 1) * (FW - (k_ + 1) // 2))
             rows = pl.ds(pl.multiple_of(i * T, T), T)
             mc = to_col(MS[H, pl.ds(i, 1), :])
             w = jnp.exp2((S[h, rows, :] - mc) * (scale * math.log2(math.e)))
             LS[i, h : h + 1, :] = to_row(jnp.sum(w, axis=1, keepdims=True))
-            O[h, i] = dot(w.astype(bf16), V[h], NN)
+            return i, w.astype(bf16)
+
+        def body(k_, carry):
+            i, w1 = weights(2 * k_)
+            j, w2 = weights(2 * k_ + 1)
+            o = dot(jnp.concatenate([w1, w2], axis=0), V[h], NN)
+            O[h, i] = o[:T]
+            O[h, j] = o[T:]
             return carry
 
         body(0, 0)
         of(h, 0)[0].start()
-        lax.fori_loop(1, 3, body, 0)
+        body(1, 0)
         ob(h, 0)[0].start()
-        lax.fori_loop(3, N, body, 0)
+        lax.fori_loop(2, N // 2, body, 0)
 
     def l_x(d):
         p = (a + d) % N
@@ -467,6 +469,11 @@
         l_x(d).wait_send()
         for h in range(H):
             m_x(h, d).wait_send()
+
+
+def copy_kernel(*refs):
+    for src, dst in zip(refs[:4], refs[4:]):
+        dst[...] = src[...]
 
 
 def per_device(mesh_shape, q, k, v, pos, qg, kg, ck, cv, cg, cot):
@@ -516,7 +523,7 @@
         dma((8 + H, MX)),
         dma((8 + H, MX)),
     ]
-    return pl.pallas_call(
+    res = pl.pallas_call(
         functools.partial(kernel, cfg),
         out_shape=out_shape,
         in_specs=[vm] * 11,
@@ -526,6 +533,9 @@
             collective_id=0, has_side_effects=True, vmem_limit_bytes=56 * 2**20
         ),
     )(q, k, v, pos.T, jnp.asarray(freq_rows()), qg, kg, ck, cv, cg, cot)
+    return pl.pallas_call(
+        copy_kernel, out_shape=out_shape, in_specs=[vm] * 4, out_specs=(vm,) * 4
+    )(*res)
 
 
 def solution(mesh):

time: 83.5 us -> 85 us (1.018); the launches traced: 82.4 us -> 84.9 us
  Pallas kernels: 77.9 us -> 84.2 us
  local copies, waits for them, and re-layouts: 3.83 us -> 0 us
    pallas_call x1, Pallas kernels: 77.9 us -> 82.5 us  [per_device(): pl.pallas_call(functools.partial(kernel, cfg), out_shape=out_shape, in_sp...]
    unnamed x10 -> x0, local copies, waits for them, and re-layouts: 3.83 us -> none
    pallas_call x0 -> x1, Pallas kernels: none -> 1.7 us  [per_device(): pl.pallas_call(copy_kernel, out_shape=out_shape, in_specs=[vm] * 4, out_s...]
where the time goes in v3:
time: 85 us; the launch traced here: 84.9 us
  Pallas kernels  84.2 us (99%)
    pallas_call x1, Pallas kernels, per_device(): pl.pallas_call(functools.partial(kernel, cfg), out_shape=out_shape, in_sp...  82.5 us

profile of v3, /device:TPU:6, one launch (start us, length us, event | category | flops | bytes accessed | tf_op | source)
XLA Modules:
  0.0 84.9 jit_solution(7517326509535699266)
XLA Ops:
  0.6 82.5 %shard_map.138 = (bf16[160,384]{1,0:T(8,128)(2,1)}, bf16[160,384]{1,0:T(8,128)(2,1)}, f32[4,3072]{1,0:T(4,128)}, f32[4,3072]{1,0:T(4,128)}) custom-call(bf16[160,384]{1,0:T(8,128)(2,1)} %q_ref.1, bf16[160,384]{1,0:T(8,128)(2,1)} %k_ref.1, bf16[160,384]{1,0:T(8,128)(2,1)} %v_ref.1, s32[3,160]{1,0:T(4,128)} %bitcast.1, f32[8,128]{1,0:T(8,128)} %constant.2.clone.fr_ref, ...), custom_call_target="tpu_custom_call" | custom-call | tf_op jit(solution)/shard_map/pallas_call | solution.py:526
  83.2 1.7 %shard_map.139 = (bf16[160,384]{1,0:T(8,128)(2,1)}, bf16[160,384]{1,0:T(8,128)(2,1)}, f32[4,3072]{1,0:T(4,128)}, f32[4,3072]{1,0:T(4,128)}) custom-call(bf16[160,384]{1,0:T(8,128)(2,1)} %get-tuple-element.8.refs_0_, bf16[160,384]{1,0:T(8,128)(2,1)} %get-tuple-element.9.refs_1_, f32[4,3072]{1,0:T(4,128)} %get-tuple-element.10.refs_2_, ...), custom_call_target="tpu_custom_call" | custom-call | tf_op jit(solution)/shard_map/pallas_call | solution.py:536

commit v4 on v3

--- a/solution.py
+++ b/solution.py
@@ -97,21 +97,26 @@
 
     def ring(i, buf, p, who, h, fwd, s):
         sg = 1 if fwd else -1
-        rows = pl.ds(pl.multiple_of(fwd_pos(p, -sg * s) * T, T), T)
+        back, hop = sg * s, sg
+        if h == 0 and fwd and s == FW - 1:
+            back, hop = 0, FW
+        rows = pl.ds(pl.multiple_of(fwd_pos(p, -back) * T, T), T)
         sl = buf.at[:, rows, :] if h is None else buf.at[h, rows, :]
         k_ = s if fwd else FW + s
         g = 0 if h is None else h
         return remote(
-            sl, sl, gs_sem.at[i, g, k_], gr_sem.at[i, g, k_], who(fwd_pos(p, sg))
+            sl, sl, gs_sem.at[i, g, k_], gr_sem.at[i, g, k_], who(fwd_pos(p, hop))
         )
 
     rings = {"q": (0, Q, a, a_dev), "k": (1, K, b, b_dev), "v": (2, V, b, b_dev)}
 
     def ring_start(t, h, s):
-        if s < FW:
+        if s < FW - 1 or (s == FW - 1 and h != 0):
             ring(*rings[t], h, True, s).start()
         if s < BW:
             ring(*rings[t], h, False, s).start()
+        if s == 0 and h == 0:
+            ring(*rings[t], h, True, FW - 1).start()
 
     def ring_recv(t, h, s):
         if s < FW:
@@ -257,10 +262,9 @@
         gsc = (pr * (gp - inner)).astype(bf16)
         gk = dot(gsc, qh, TN) * scale
         both = jnp.where(is_key_s, gk, pltpu.roll(gv, 4, 0))
-        for r in range(R):
-            for j in range(E):
-                lo = (r * E + j) * 8
-                G1s[j, r, :, hs] = both[lo : lo + 8, :]
+        for j in range(E):
+            rows = [both[(r * E + j) * 8 : (r * E + j + 1) * 8, :] for r in range(R)]
+            G1s[j, :, hs] = jnp.concatenate(rows, axis=0).astype(bf16)
 
     for h in range(H):
         image_head(h)
@@ -382,10 +386,10 @@
         if h == 0:
             for d in range(1, N):
                 g1_x(d).wait_recv()
-            g = G1[0]
+            g = G1[0].astype(f32)
             for j in range(1, N):
-                g = g + G1[j]
-            G2s[...] = g
+                g = g + G1[j].astype(f32)
+            G2s[...] = g.reshape(R, 8, W)
             for d in range(1, N):
                 g2_x(d).start()
             G2[y] = G2s[row]
@@ -508,8 +512,8 @@
         pltpu.VMEM((H, N, N, T), f32),
         pltpu.VMEM((N, 8, T), f32),
         pltpu.VMEM((N, 8, T), f32),
-        pltpu.VMEM((N, R, 8, W), f32),
-        pltpu.VMEM((N, R, 8, W), f32),
+        pltpu.VMEM((N, R * 8, W), bf16),
+        pltpu.VMEM((N, R * 8, W), bf16),
         pltpu.VMEM((R, 8, W), f32),
         pltpu.VMEM((N, 8, W), f32),
         pltpu.VMEM((N, 8, W), f32),

time: 85 us -> 82.2 us (0.967)
  Pallas kernels: 84.2 us -> 81 us
    pallas_call x1, Pallas kernels: 82.5 us -> 79.3 us  [per_device(): pl.pallas_call(functools.partial(kernel, cfg), out_shape=out_shape, in_sp...]
where the time goes in v4:
time: 82.2 us; the launch traced here: 81.6 us
  Pallas kernels  81 us (99%)
    pallas_call x1, Pallas kernels, per_device(): pl.pallas_call(functools.partial(kernel, cfg), out_shape=out_shape, in_sp...  79.3 us
    pallas_call x1, Pallas kernels, per_device(): pl.pallas_call(copy_kernel, out_shape=out_shape, in_specs=[vm] * 4, out_s...  1.7 us

profile of v4, /device:TPU:6, one launch (start us, length us, event | category | flops | bytes accessed | tf_op | source)
XLA Modules:
  0.0 81.6 jit_solution(13390204451734131358)
XLA Ops:
  0.6 79.3 %shard_map.138 = (bf16[160,384]{1,0:T(8,128)(2,1)}, bf16[160,384]{1,0:T(8,128)(2,1)}, f32[4,3072]{1,0:T(4,128)}, f32[4,3072]{1,0:T(4,128)}) custom-call(bf16[160,384]{1,0:T(8,128)(2,1)} %q_ref.1, bf16[160,384]{1,0:T(8,128)(2,1)} %k_ref.1, bf16[160,384]{1,0:T(8,128)(2,1)} %v_ref.1, s32[3,160]{1,0:T(4,128)} %bitcast.1, f32[8,128]{1,0:T(8,128)} %constant.2.clone.fr_ref, ...), custom_call_target="tpu_custom_call" | custom-call | tf_op jit(solution)/shard_map/pallas_call | solution.py:530
  79.9 1.7 %shard_map.139 = (bf16[160,384]{1,0:T(8,128)(2,1)}, bf16[160,384]{1,0:T(8,128)(2,1)}, f32[4,3072]{1,0:T(4,128)}, f32[4,3072]{1,0:T(4,128)}) custom-call(bf16[160,384]{1,0:T(8,128)(2,1)} %get-tuple-element.8.refs_0_, bf16[160,384]{1,0:T(8,128)(2,1)} %get-tuple-element.9.refs_1_, f32[4,3072]{1,0:T(4,128)} %get-tuple-element.10.refs_2_, ...), custom_call_target="tpu_custom_call" | custom-call | tf_op jit(solution)/shard_map/pallas_call | solution.py:540

commit v5 on v3

--- a/solution.py
+++ b/solution.py
@@ -97,21 +97,26 @@
 
     def ring(i, buf, p, who, h, fwd, s):
         sg = 1 if fwd else -1
-        rows = pl.ds(pl.multiple_of(fwd_pos(p, -sg * s) * T, T), T)
+        back, hop = sg * s, sg
+        if h == 0 and fwd and s == FW - 1:
+            back, hop = 0, FW
+        rows = pl.ds(pl.multiple_of(fwd_pos(p, -back) * T, T), T)
         sl = buf.at[:, rows, :] if h is None else buf.at[h, rows, :]
         k_ = s if fwd else FW + s
         g = 0 if h is None else h
         return remote(
-            sl, sl, gs_sem.at[i, g, k_], gr_sem.at[i, g, k_], who(fwd_pos(p, sg))
+            sl, sl, gs_sem.at[i, g, k_], gr_sem.at[i, g, k_], who(fwd_pos(p, hop))
         )
 
     rings = {"q": (0, Q, a, a_dev), "k": (1, K, b, b_dev), "v": (2, V, b, b_dev)}
 
     def ring_start(t, h, s):
-        if s < FW:
+        if s < FW - 1 or (s == FW - 1 and h != 0):
             ring(*rings[t], h, True, s).start()
         if s < BW:
             ring(*rings[t], h, False, s).start()
+        if s == 0 and h == 0:
+            ring(*rings[t], h, True, FW - 1).start()
 
     def ring_recv(t, h, s):
         if s < FW:
@@ -379,7 +384,7 @@
         pass2(h)
         for j in range(h, -1, -1):
             o_step(j, h - j + 1)
-        if h == 0:
+        if h == max(H - 2, 0):
             for d in range(1, N):
                 g1_x(d).wait_recv()
             g = G1[0]

time: 85 us -> 87.4 us (1.028)
  Pallas kernels: 84.2 us -> 85.8 us
    pallas_call x1, Pallas kernels: 82.5 us -> 84.1 us  [per_device(): pl.pallas_call(functools.partial(kernel, cfg), out_shape=out_shape, in_sp...]
where the time goes in v5:
time: 87.4 us; the launch traced here: 86.4 us
  Pallas kernels  85.8 us (98%)
    pallas_call x1, Pallas kernels, per_device(): pl.pallas_call(functools.partial(kernel, cfg), out_shape=out_shape, in_sp...  84.1 us

profile of v5, /device:TPU:6, one launch (start us, length us, event | category | flops | bytes accessed | tf_op | source)
XLA Modules:
  0.0 86.4 jit_solution(2138747401158729626)
XLA Ops:
  0.6 84.1 %shard_map.138 = (bf16[160,384]{1,0:T(8,128)(2,1)}, bf16[160,384]{1,0:T(8,128)(2,1)}, f32[4,3072]{1,0:T(4,128)}, f32[4,3072]{1,0:T(4,128)}) custom-call(bf16[160,384]{1,0:T(8,128)(2,1)} %q_ref.1, bf16[160,384]{1,0:T(8,128)(2,1)} %k_ref.1, bf16[160,384]{1,0:T(8,128)(2,1)} %v_ref.1, s32[3,160]{1,0:T(4,128)} %bitcast.1, f32[8,128]{1,0:T(8,128)} %constant.2.clone.fr_ref, ...), custom_call_target="tpu_custom_call" | custom-call | tf_op jit(solution)/shard_map/pallas_call | solution.py:531
  84.7 1.7 %shard_map.139 = (bf16[160,384]{1,0:T(8,128)(2,1)}, bf16[160,384]{1,0:T(8,128)(2,1)}, f32[4,3072]{1,0:T(4,128)}, f32[4,3072]{1,0:T(4,128)}) custom-call(bf16[160,384]{1,0:T(8,128)(2,1)} %get-tuple-element.8.refs_0_, bf16[160,384]{1,0:T(8,128)(2,1)} %get-tuple-element.9.refs_1_, f32[4,3072]{1,0:T(4,128)} %get-tuple-element.10.refs_2_, ...), custom_call_target="tpu_custom_call" | custom-call | tf_op jit(solution)/shard_map/pallas_call | solution.py:541
